TPU v7x, 512 devices: a whole 4x8x8 slice. The times are simulated.
512 devices in a mesh: prompt: 32 (over y_lo, x, core), ctx: 16 (over z, y_hi).
Axes of the slice: x: 4, y: 8 (y_hi: 2, y_lo: 4; y = y_hi * 4 + y_lo), z: 8, core: 2. Of those that a mesh axis runs over, the one named last changes fastest.
Arguments:
- prefix_qkv: bfloat16 [32, 2048, 768], P('prompt', 'ctx'), may hold values from -8 to 8
- rollout: bfloat16 [32, 16, 32, 32, 768], P('prompt', 'ctx'), may hold values from -8 to 8
- arrival_order: int32 [32, 16, 1024], P('prompt', 'ctx'), may hold values from 0 to 1023, each once within a row
- resp_len: int32 [32, 32], P('prompt', 'ctx'), may hold values from 1 to 512, 10240 in all within a row
Outputs:
- prefix_out: bfloat16 [32, 2048, 512], P('prompt', 'ctx')
- resp_out: bfloat16 [32, 32, 512, 512], P('prompt', 'ctx')
All inputs are finite; a program needn't handle non-finite values. No bound on the sum of `resp_len` on one device may be relied on, other than what follows from the above.
Results may differ from a plain program's by a relative error of at most 0.0075.
Values may be sent and summed in bfloat16 or wider, within the bound.
A program may use at most 64 MiB of HBM per device.

v0:
```python
import math

import jax
import jax.numpy as jnp
from jax import lax
from jax.sharding import PartitionSpec as P

HEAD = 128
RESP_DEV = 2


MASKED_SCORE = -1e30


def shifted(x, axis, by):
    peers = lax.axis_size(axis)
    return lax.ppermute(x, axis, [(i, (i + by) % peers) for i in range(peers)])


def absorb(state, queries, key_rows, values, allowed):
    row_max, row_sum, weighted = state
    scores = jnp.einsum(
        "rhd,kd->hrk", queries, key_rows, preferred_element_type=jnp.float32
    ) * HEAD ** (-0.5)
    scores = jnp.where(allowed[None], scores, MASKED_SCORE)
    new_max = jnp.maximum(row_max, jnp.max(scores, axis=-1))
    weights = jnp.exp(scores - new_max[..., None])
    rescale = jnp.exp(row_max - new_max)
    row_sum = row_sum * rescale + jnp.sum(weights, axis=-1)
    weighted = weighted * rescale[..., None] + jnp.einsum(
        "hrk,kd->hrd", weights.astype(jnp.bfloat16), values, preferred_element_type=jnp.float32
    )
    return (new_max, row_sum, weighted)


def empty_state(head_count, row_count):
    return (
        jnp.full((head_count, row_count), MASKED_SCORE, jnp.float32),
        jnp.zeros((head_count, row_count), jnp.float32),
        jnp.zeros((head_count, row_count, HEAD), jnp.float32),
    )


def finish(state):
    row_max, row_sum, weighted = state
    result = weighted / row_sum[..., None]
    head_count, row_count, head_size = result.shape
    return jnp.transpose(result, (1, 0, 2)).reshape(row_count, head_count * head_size)


def body(prefix_qkv, rollout, arrival_order, resp_len):
    ctx_count = lax.axis_size("ctx")
    ctx_index = lax.axis_index("ctx")
    prefix_rows = prefix_qkv[0]
    prefix_len = prefix_rows.shape[0]
    query_span = prefix_rows.shape[1] - 2 * HEAD
    head_count = query_span // HEAD
    prefix_kv = prefix_rows[:, query_span:]
    own_low = ctx_index * prefix_len
    row_order = arrival_order[0, 0]
    arrived = lax.all_to_all(rollout, "prompt", split_axis=2, concat_axis=0, tiled=True)
    arrived_rows = arrived.reshape(-1, arrived.shape[-1])
    placed = jnp.take(arrived_rows, row_order, axis=0)
    resp_rows = placed.shape[0]
    resp_start = empty_state(head_count, resp_rows)
    slot_len = resp_rows // RESP_DEV
    prefix_queries = prefix_rows[:, :query_span].reshape(prefix_len, head_count, HEAD)
    resp_queries = placed[:, :query_span].reshape(resp_rows, head_count, HEAD)
    prefix_pos = own_low + jnp.arange(prefix_len)

    def fold_piece(states, piece, start):
        piece_rows = piece.shape[0]
        block_size = math.gcd(piece_rows, 128)
        open_mask = jnp.ones((resp_rows, block_size), dtype=bool)

        def absorb_block(i, carried):
            prefix_state, resp_state = carried
            key_rows = piece[:, :HEAD]
            values = piece[:, HEAD:]
            block_start = start + i * block_size
            key_pos = block_start + jnp.arange(block_size)
            prefix_state = absorb(
                prefix_state,
                prefix_queries,
                key_rows,
                values,
                key_pos[None, :] <= prefix_pos[:, None],
            )
            resp_state = absorb(resp_state, resp_queries, key_rows, values, open_mask)
            return (prefix_state, resp_state)

        return lax.fori_loop(0, piece_rows // block_size, absorb_block, states)

    states = (empty_state(head_count, prefix_len), resp_start)
    states = fold_piece(states, prefix_kv, own_low)

    def loop_turn(t, carried):
        fold_states, held_piece = carried
        held_piece = shifted(held_piece, "ctx", 1)
        source_index = (ctx_index - t) % ctx_count
        fold_states = fold_piece(fold_states, held_piece, source_index * prefix_len)
        return (fold_states, held_piece)

    states, held_final = lax.fori_loop(1, ctx_count, loop_turn, (states, prefix_kv))
    prefix_state, resp_state = states
    own_pos = jnp.arange(slot_len)
    own_causal = own_pos[None, :] <= own_pos[:, None]
    resp_parts = []
    for index_resp in range(RESP_DEV):
        first_row = index_resp * slot_len
        sub_state = tuple(
            (
                lax.slice_in_dim(member, first_row, first_row + slot_len, axis=1)
                for member in resp_state
            )
        )
        own_rows = placed[first_row : first_row + slot_len]
        sub_state = absorb(
            sub_state,
            resp_queries[first_row : first_row + slot_len],
            own_rows[:, query_span : query_span + HEAD],
            own_rows[:, query_span + HEAD :],
            own_causal,
        )
        weighted = finish(sub_state)
        live_rows = (own_pos < resp_len[0, index_resp])[:, None]
        resp_parts.append(jnp.where(live_rows, weighted, 0.0).astype(jnp.bfloat16))
    resp_out = jnp.stack(resp_parts, axis=0)[None]
    prefix_out = finish(prefix_state).astype(jnp.bfloat16)[None]
    return (prefix_out, resp_out)


def solution(mesh):
    placed = (
        P("prompt", "ctx", None),
        P("prompt", "ctx", None, None, None),
        P("prompt", "ctx", None),
        P("prompt", "ctx"),
    )
    return jax.shard_map(
        body,
        mesh=mesh,
        in_specs=placed,
        out_specs=(P("prompt", "ctx", None), P("prompt", "ctx", None, None)),
        check_vma=False,
    )
```

profile of v0, /device:TPU:10, one launch (start us, length us, event | category | flops | bytes accessed | tf_op | source)
XLA Modules:
  0.0 334.9 jit_solution(13391271310324466914)
XLA Ops:
  0.7 9.6 %all-to-all-start = ((bf16[1,1,32,32,768]{4,3,1,0,2:T(8,128)(2,1)}), bf16[1,1,32,32,768]{4,3,1,0,2:T(8,128)(2,1)S(1)}, u32[]{:S(2)}, u32[]{:S(2)}) async-start(bf16[1,1,32,32,768]{4,3,1,0,2:T(8,128)(2,1)} %bitcast.150), calls=%async_computation | async-start | bytes 3145728 | tf_op jit(solution)/shard_map/all_to_all | solution.py:61
  15.3 30.6 %all-to-all-done = bf16[1,1,32,32,768]{4,3,1,0,2:T(8,128)(2,1)S(1)} async-done(((bf16[1,1,32,32,768]{4,3,1,0,2:T(8,128)(2,1)}), bf16[1,1,32,32,768]{4,3,1,0,2:T(8,128)(2,1)S(1)}, u32[]{:S(2)}, u32[]{:S(2)}) %all-to-all-start) | async-done | bytes 1572896 | tf_op jit(solution)/shard_map/all_to_all | solution.py:61
  45.9 4.0 %gather_fusion = bf16[1024,768]{1,0:T(8,128)(2,1)S(1)} fusion(bf16[1024,768]{1,0:T(8,128)(2,1)S(1)} %bitcast.146, s32[1024]{0:T(1024)S(1)} %broadcast_clamp_fusion), kind=kCustom, calls=%fused_computation | custom fusion | bytes 3149824 | tf_op jit(solution)/shard_map/jit(_take)/gather | solution.py:63
  54.5 1.7 bitcast_reduce_fusion.1
  56.2 2.4 copy.55
  59.1 2.3 convolution_add_fusion.1
  61.3 257.1 %while.62 = (s32[]{:T(128)}, f32[4,128]{1,0:T(4,128)S(1)}, f32[4,128]{1,0:T(4,128)S(1)}, f32[4,128,128]{2,1,0:T(8,128)S(1)}, f32[4,1024]{1,0:T(4,128)S(1)}, /*in...) while((s32[]{:T(128)}, f32[4,128]{1,0:T(4,128)S(1)}, ...), condition=%wide.region_9.10_spmd.clone, body=%wide.region_4.9_spmd.clone.sunk | while | flops 307848448 | bytes 13830482 | solution.py:104
  61.4 3.4 %collective-permute-start = (bf16[128,256]{1,0:T(8,128)(2,1)}, bf16[128,256]{1,0:T(8,128)(2,1)S(1)}, u32[]{:S(2)}, u32[]{:S(2)}) collective-permute-start(bf16[128,256]{1,0:T(8,128)(2,1)} %get-tuple-element.629), channel_id=1, source_target_pairs={{0,1},{1,2},{2,3},{3,4},{4,5},{5,6},{6,7},{7,8},{8,9},{9,10},{10,1... | collective-permute-start | bytes 196616 | tf_op jit(solution)/shard_map/while/body/eval_jaxpr/ppermute | solution.py:17
  64.9 12.8 %collective-permute-done = bf16[128,256]{1,0:T(8,128)(2,1)S(1)} collective-permute-done((bf16[128,256]{1,0:T(8,128)(2,1)}, bf16[128,256]{1,0:T(8,128)(2,1)S(1)}, u32[]{:S(2)}, u32[]{:S(2)}) %collective-permute-start) | collective-permute-done | bytes 65568 | tf_op jit(solution)/shard_map/while/body/eval_jaxpr/ppermute | solution.py:17
  77.7 1.1 fusion.85
  80.7 1.2 multiply_add_fusion.10
  82.0 1.9 collective-permute-start
  84.0 10.8 %collective-permute-done = bf16[128,256]{1,0:T(8,128)(2,1)S(1)} collective-permute-done((bf16[128,256]{1,0:T(8,128)(2,1)}, bf16[128,256]{1,0:T(8,128)(2,1)S(1)}, u32[]{:S(2)}, u32[]{:S(2)}) %collective-permute-start) | collective-permute-done | bytes 65568 | tf_op jit(solution)/shard_map/while/body/eval_jaxpr/ppermute | solution.py:17
  94.8 1.1 fusion.85
  97.8 1.3 multiply_add_fusion.10
  99.1 1.9 collective-permute-start
  101.1 10.3 %collective-permute-done = bf16[128,256]{1,0:T(8,128)(2,1)S(1)} collective-permute-done((bf16[128,256]{1,0:T(8,128)(2,1)}, bf16[128,256]{1,0:T(8,128)(2,1)S(1)}, u32[]{:S(2)}, u32[]{:S(2)}) %collective-permute-start) | collective-permute-done | bytes 65568 | tf_op jit(solution)/shard_map/while/body/eval_jaxpr/ppermute | solution.py:17
  114.5 1.2 multiply_add_fusion.10
  115.7 1.9 collective-permute-start
  117.8 10.4 %collective-permute-done = bf16[128,256]{1,0:T(8,128)(2,1)S(1)} collective-permute-done((bf16[128,256]{1,0:T(8,128)(2,1)}, bf16[128,256]{1,0:T(8,128)(2,1)S(1)}, u32[]{:S(2)}, u32[]{:S(2)}) %collective-permute-start) | collective-permute-done | bytes 65568 | tf_op jit(solution)/shard_map/while/body/eval_jaxpr/ppermute | solution.py:17
  131.1 1.2 multiply_add_fusion.10
  132.4 1.9 collective-permute-start
  134.4 11.0 %collective-permute-done = bf16[128,256]{1,0:T(8,128)(2,1)S(1)} collective-permute-done((bf16[128,256]{1,0:T(8,128)(2,1)}, bf16[128,256]{1,0:T(8,128)(2,1)S(1)}, u32[]{:S(2)}, u32[]{:S(2)}) %collective-permute-start) | collective-permute-done | bytes 65568 | tf_op jit(solution)/shard_map/while/body/eval_jaxpr/ppermute | solution.py:17
  148.5 1.2 multiply_add_fusion.10
  149.7 1.9 collective-permute-start
  151.8 10.6 %collective-permute-done = bf16[128,256]{1,0:T(8,128)(2,1)S(1)} collective-permute-done((bf16[128,256]{1,0:T(8,128)(2,1)}, bf16[128,256]{1,0:T(8,128)(2,1)S(1)}, u32[]{:S(2)}, u32[]{:S(2)}) %collective-permute-start) | collective-permute-done | bytes 65568 | tf_op jit(solution)/shard_map/while/body/eval_jaxpr/ppermute | solution.py:17
  162.4 1.1 fusion.85
  165.3 1.2 multiply_add_fusion.10
  166.6 1.9 collective-permute-start
  168.7 10.3 %collective-permute-done = bf16[128,256]{1,0:T(8,128)(2,1)S(1)} collective-permute-done((bf16[128,256]{1,0:T(8,128)(2,1)}, bf16[128,256]{1,0:T(8,128)(2,1)S(1)}, u32[]{:S(2)}, u32[]{:S(2)}) %collective-permute-start) | collective-permute-done | bytes 65568 | tf_op jit(solution)/shard_map/while/body/eval_jaxpr/ppermute | solution.py:17
  179.0 1.1 fusion.85
  182.0 1.3 multiply_add_fusion.10
  183.2 1.9 collective-permute-start
  185.3 10.3 %collective-permute-done = bf16[128,256]{1,0:T(8,128)(2,1)S(1)} collective-permute-done((bf16[128,256]{1,0:T(8,128)(2,1)}, bf16[128,256]{1,0:T(8,128)(2,1)S(1)}, u32[]{:S(2)}, u32[]{:S(2)}) %collective-permute-start) | collective-permute-done | bytes 65568 | tf_op jit(solution)/shard_map/while/body/eval_jaxpr/ppermute | solution.py:17
  195.6 1.1 fusion.85
  198.6 1.2 multiply_add_fusion.10
  199.9 1.9 collective-permute-start
  201.9 10.3 %collective-permute-done = bf16[128,256]{1,0:T(8,128)(2,1)S(1)} collective-permute-done((bf16[128,256]{1,0:T(8,128)(2,1)}, bf16[128,256]{1,0:T(8,128)(2,1)S(1)}, u32[]{:S(2)}, u32[]{:S(2)}) %collective-permute-start) | collective-permute-done | bytes 65568 | tf_op jit(solution)/shard_map/while/body/eval_jaxpr/ppermute | solution.py:17
  215.3 1.3 multiply_add_fusion.10
  216.5 1.9 collective-permute-start
  218.6 10.3 %collective-permute-done = bf16[128,256]{1,0:T(8,128)(2,1)S(1)} collective-permute-done((bf16[128,256]{1,0:T(8,128)(2,1)}, bf16[128,256]{1,0:T(8,128)(2,1)S(1)}, u32[]{:S(2)}, u32[]{:S(2)}) %collective-permute-start) | collective-permute-done | bytes 65568 | tf_op jit(solution)/shard_map/while/body/eval_jaxpr/ppermute | solution.py:17
  228.9 1.1 fusion.85
  231.9 1.3 multiply_add_fusion.10
  233.2 1.9 collective-permute-start
  235.2 10.3 %collective-permute-done = bf16[128,256]{1,0:T(8,128)(2,1)S(1)} collective-permute-done((bf16[128,256]{1,0:T(8,128)(2,1)}, bf16[128,256]{1,0:T(8,128)(2,1)S(1)}, u32[]{:S(2)}, u32[]{:S(2)}) %collective-permute-start) | collective-permute-done | bytes 65568 | tf_op jit(solution)/shard_map/while/body/eval_jaxpr/ppermute | solution.py:17
  245.6 1.1 fusion.85
  248.5 1.2 multiply_add_fusion.10
  249.8 1.9 collective-permute-start
  251.9 11.8 %collective-permute-done = bf16[128,256]{1,0:T(8,128)(2,1)S(1)} collective-permute-done((bf16[128,256]{1,0:T(8,128)(2,1)}, bf16[128,256]{1,0:T(8,128)(2,1)S(1)}, u32[]{:S(2)}, u32[]{:S(2)}) %collective-permute-start) | collective-permute-done | bytes 65568 | tf_op jit(solution)/shard_map/while/body/eval_jaxpr/ppermute | solution.py:17
  266.7 1.3 multiply_add_fusion.10
  268.0 1.9 collective-permute-start
  270.0 10.9 %collective-permute-done = bf16[128,256]{1,0:T(8,128)(2,1)S(1)} collective-permute-done((bf16[128,256]{1,0:T(8,128)(2,1)}, bf16[128,256]{1,0:T(8,128)(2,1)S(1)}, u32[]{:S(2)}, u32[]{:S(2)}) %collective-permute-start) | collective-permute-done | bytes 65568 | tf_op jit(solution)/shard_map/while/body/eval_jaxpr/ppermute | solution.py:17
  283.8 1.2 multiply_add_fusion.10
  285.1 1.9 collective-permute-start
  287.2 10.4 %collective-permute-done = bf16[128,256]{1,0:T(8,128)(2,1)S(1)} collective-permute-done((bf16[128,256]{1,0:T(8,128)(2,1)}, bf16[128,256]{1,0:T(8,128)(2,1)S(1)}, u32[]{:S(2)}, u32[]{:S(2)}) %collective-permute-start) | collective-permute-done | bytes 65568 | tf_op jit(solution)/shard_map/while/body/eval_jaxpr/ppermute | solution.py:17
  300.5 1.2 multiply_add_fusion.10
  301.8 1.9 collective-permute-start
  303.8 10.3 %collective-permute-done = bf16[128,256]{1,0:T(8,128)(2,1)S(1)} collective-permute-done((bf16[128,256]{1,0:T(8,128)(2,1)}, bf16[128,256]{1,0:T(8,128)(2,1)S(1)}, u32[]{:S(2)}, u32[]{:S(2)}) %collective-permute-start) | collective-permute-done | bytes 65568 | tf_op jit(solution)/shard_map/while/body/eval_jaxpr/ppermute | solution.py:17
  317.2 1.3 multiply_add_fusion.10
  319.4 1.9 copy.54
  321.3 1.8 fusion.20
  323.1 2.9 fusion.16
  327.6 2.1 fusion.42
  329.9 3.3 fusion.45
  (262 shorter events, 51.7 us)
Async XLA Ops:
  0.6 9.6 %copy-start.7 = (bf16[1,128,768]{2,1,0:T(8,128)(2,1)S(1)}, bf16[1,128,768]{2,1,0:T(8,128)(2,1)}, u32[]{:S(2)}) copy-start(bf16[1,128,768]{2,1,0:T(8,128)(2,1)} %param.6) | copy-start | bytes 589828
  0.6 11.2 %copy-start.10 = (s32[1,2]{1,0:T(1,128)S(1)}, s32[1,2]{1,0:T(1,128)}, u32[]{:S(2)}) copy-start(s32[1,2]{1,0:T(1,128)} %param.9) | copy-start | bytes 28
  0.7 14.3 %copy-start.9 = (s32[1,1,1024]{2,1,0:T(1,128)S(1)}, s32[1,1,1024]{2,1,0:T(1,128)}, u32[]{:S(2)}) copy-start(s32[1,1,1024]{2,1,0:T(1,128)} %param.8) | copy-start | bytes 12292
  0.7 45.2 %all-to-all-start = ((bf16[1,1,32,32,768]{4,3,1,0,2:T(8,128)(2,1)}), bf16[1,1,32,32,768]{4,3,1,0,2:T(8,128)(2,1)S(1)}, u32[]{:S(2)}, u32[]{:S(2)}) async-start(bf16[1,1,32,32,768]{4,3,1,0,2:T(8,128)(2,1)} %bitcast.150), calls=%async_computation | async-start | bytes 3145728 | tf_op jit(solution)/shard_map/all_to_all | solution.py:61
  50.1 1.1 copy-start.2
  52.9 1.0 copy-start.1
  56.2 2.8 copy-start
  61.4 16.4 %collective-permute-start = (bf16[128,256]{1,0:T(8,128)(2,1)}, bf16[128,256]{1,0:T(8,128)(2,1)S(1)}, u32[]{:S(2)}, u32[]{:S(2)}) collective-permute-start(bf16[128,256]{1,0:T(8,128)(2,1)} %get-tuple-element.629), channel_id=1, source_target_pairs={{0,1},{1,2},{2,3},{3,4},{4,5},{5,6},{6,7},{7,8},{8,9},{9,10},{10,1... | collective-permute-start | bytes 196616 | tf_op jit(solution)/shard_map/while/body/eval_jaxpr/ppermute | solution.py:17
  82.0 12.9 %collective-permute-start = (bf16[128,256]{1,0:T(8,128)(2,1)}, bf16[128,256]{1,0:T(8,128)(2,1)S(1)}, u32[]{:S(2)}, u32[]{:S(2)}) collective-permute-start(bf16[128,256]{1,0:T(8,128)(2,1)} %get-tuple-element.629), channel_id=1, source_target_pairs={{0,1},{1,2},{2,3},{3,4},{4,5},{5,6},{6,7},{7,8},{8,9},{9,10},{10,1... | collective-permute-start | bytes 196616 | tf_op jit(solution)/shard_map/while/body/eval_jaxpr/ppermute | solution.py:17
  99.1 12.4 %collective-permute-start = (bf16[128,256]{1,0:T(8,128)(2,1)}, bf16[128,256]{1,0:T(8,128)(2,1)S(1)}, u32[]{:S(2)}, u32[]{:S(2)}) collective-permute-start(bf16[128,256]{1,0:T(8,128)(2,1)} %get-tuple-element.629), channel_id=1, source_target_pairs={{0,1},{1,2},{2,3},{3,4},{4,5},{5,6},{6,7},{7,8},{8,9},{9,10},{10,1... | collective-permute-start | bytes 196616 | tf_op jit(solution)/shard_map/while/body/eval_jaxpr/ppermute | solution.py:17
  115.7 12.4 %collective-permute-start = (bf16[128,256]{1,0:T(8,128)(2,1)}, bf16[128,256]{1,0:T(8,128)(2,1)S(1)}, u32[]{:S(2)}, u32[]{:S(2)}) collective-permute-start(bf16[128,256]{1,0:T(8,128)(2,1)} %get-tuple-element.629), channel_id=1, source_target_pairs={{0,1},{1,2},{2,3},{3,4},{4,5},{5,6},{6,7},{7,8},{8,9},{9,10},{10,1... | collective-permute-start | bytes 196616 | tf_op jit(solution)/shard_map/while/body/eval_jaxpr/ppermute | solution.py:17
  132.4 13.1 %collective-permute-start = (bf16[128,256]{1,0:T(8,128)(2,1)}, bf16[128,256]{1,0:T(8,128)(2,1)S(1)}, u32[]{:S(2)}, u32[]{:S(2)}) collective-permute-start(bf16[128,256]{1,0:T(8,128)(2,1)} %get-tuple-element.629), channel_id=1, source_target_pairs={{0,1},{1,2},{2,3},{3,4},{4,5},{5,6},{6,7},{7,8},{8,9},{9,10},{10,1... | collective-permute-start | bytes 196616 | tf_op jit(solution)/shard_map/while/body/eval_jaxpr/ppermute | solution.py:17
  149.7 12.6 %collective-permute-start = (bf16[128,256]{1,0:T(8,128)(2,1)}, bf16[128,256]{1,0:T(8,128)(2,1)S(1)}, u32[]{:S(2)}, u32[]{:S(2)}) collective-permute-start(bf16[128,256]{1,0:T(8,128)(2,1)} %get-tuple-element.629), channel_id=1, source_target_pairs={{0,1},{1,2},{2,3},{3,4},{4,5},{5,6},{6,7},{7,8},{8,9},{9,10},{10,1... | collective-permute-start | bytes 196616 | tf_op jit(solution)/shard_map/while/body/eval_jaxpr/ppermute | solution.py:17
  166.6 12.4 %collective-permute-start = (bf16[128,256]{1,0:T(8,128)(2,1)}, bf16[128,256]{1,0:T(8,128)(2,1)S(1)}, u32[]{:S(2)}, u32[]{:S(2)}) collective-permute-start(bf16[128,256]{1,0:T(8,128)(2,1)} %get-tuple-element.629), channel_id=1, source_target_pairs={{0,1},{1,2},{2,3},{3,4},{4,5},{5,6},{6,7},{7,8},{8,9},{9,10},{10,1... | collective-permute-start | bytes 196616 | tf_op jit(solution)/shard_map/while/body/eval_jaxpr/ppermute | solution.py:17
  183.2 12.4 %collective-permute-start = (bf16[128,256]{1,0:T(8,128)(2,1)}, bf16[128,256]{1,0:T(8,128)(2,1)S(1)}, u32[]{:S(2)}, u32[]{:S(2)}) collective-permute-start(bf16[128,256]{1,0:T(8,128)(2,1)} %get-tuple-element.629), channel_id=1, source_target_pairs={{0,1},{1,2},{2,3},{3,4},{4,5},{5,6},{6,7},{7,8},{8,9},{9,10},{10,1... | collective-permute-start | bytes 196616 | tf_op jit(solution)/shard_map/while/body/eval_jaxpr/ppermute | solution.py:17
  199.9 12.4 %collective-permute-start = (bf16[128,256]{1,0:T(8,128)(2,1)}, bf16[128,256]{1,0:T(8,128)(2,1)S(1)}, u32[]{:S(2)}, u32[]{:S(2)}) collective-permute-start(bf16[128,256]{1,0:T(8,128)(2,1)} %get-tuple-element.629), channel_id=1, source_target_pairs={{0,1},{1,2},{2,3},{3,4},{4,5},{5,6},{6,7},{7,8},{8,9},{9,10},{10,1... | collective-permute-start | bytes 196616 | tf_op jit(solution)/shard_map/while/body/eval_jaxpr/ppermute | solution.py:17
  216.5 12.4 %collective-permute-start = (bf16[128,256]{1,0:T(8,128)(2,1)}, bf16[128,256]{1,0:T(8,128)(2,1)S(1)}, u32[]{:S(2)}, u32[]{:S(2)}) collective-permute-start(bf16[128,256]{1,0:T(8,128)(2,1)} %get-tuple-element.629), channel_id=1, source_target_pairs={{0,1},{1,2},{2,3},{3,4},{4,5},{5,6},{6,7},{7,8},{8,9},{9,10},{10,1... | collective-permute-start | bytes 196616 | tf_op jit(solution)/shard_map/while/body/eval_jaxpr/ppermute | solution.py:17
  233.2 12.4 %collective-permute-start = (bf16[128,256]{1,0:T(8,128)(2,1)}, bf16[128,256]{1,0:T(8,128)(2,1)S(1)}, u32[]{:S(2)}, u32[]{:S(2)}) collective-permute-start(bf16[128,256]{1,0:T(8,128)(2,1)} %get-tuple-element.629), channel_id=1, source_target_pairs={{0,1},{1,2},{2,3},{3,4},{4,5},{5,6},{6,7},{7,8},{8,9},{9,10},{10,1... | collective-permute-start | bytes 196616 | tf_op jit(solution)/shard_map/while/body/eval_jaxpr/ppermute | solution.py:17
  249.8 13.9 %collective-permute-start = (bf16[128,256]{1,0:T(8,128)(2,1)}, bf16[128,256]{1,0:T(8,128)(2,1)S(1)}, u32[]{:S(2)}, u32[]{:S(2)}) collective-permute-start(bf16[128,256]{1,0:T(8,128)(2,1)} %get-tuple-element.629), channel_id=1, source_target_pairs={{0,1},{1,2},{2,3},{3,4},{4,5},{5,6},{6,7},{7,8},{8,9},{9,10},{10,1... | collective-permute-start | bytes 196616 | tf_op jit(solution)/shard_map/while/body/eval_jaxpr/ppermute | solution.py:17
  268.0 12.9 %collective-permute-start = (bf16[128,256]{1,0:T(8,128)(2,1)}, bf16[128,256]{1,0:T(8,128)(2,1)S(1)}, u32[]{:S(2)}, u32[]{:S(2)}) collective-permute-start(bf16[128,256]{1,0:T(8,128)(2,1)} %get-tuple-element.629), channel_id=1, source_target_pairs={{0,1},{1,2},{2,3},{3,4},{4,5},{5,6},{6,7},{7,8},{8,9},{9,10},{10,1... | collective-permute-start | bytes 196616 | tf_op jit(solution)/shard_map/while/body/eval_jaxpr/ppermute | solution.py:17
  285.1 12.4 %collective-permute-start = (bf16[128,256]{1,0:T(8,128)(2,1)}, bf16[128,256]{1,0:T(8,128)(2,1)S(1)}, u32[]{:S(2)}, u32[]{:S(2)}) collective-permute-start(bf16[128,256]{1,0:T(8,128)(2,1)} %get-tuple-element.629), channel_id=1, source_target_pairs={{0,1},{1,2},{2,3},{3,4},{4,5},{5,6},{6,7},{7,8},{8,9},{9,10},{10,1... | collective-permute-start | bytes 196616 | tf_op jit(solution)/shard_map/while/body/eval_jaxpr/ppermute | solution.py:17
  301.8 12.4 %collective-permute-start = (bf16[128,256]{1,0:T(8,128)(2,1)}, bf16[128,256]{1,0:T(8,128)(2,1)S(1)}, u32[]{:S(2)}, u32[]{:S(2)}) collective-permute-start(bf16[128,256]{1,0:T(8,128)(2,1)} %get-tuple-element.629), channel_id=1, source_target_pairs={{0,1},{1,2},{2,3},{3,4},{4,5},{5,6},{6,7},{7,8},{8,9},{9,10},{10,1... | collective-permute-start | bytes 196616 | tf_op jit(solution)/shard_map/while/body/eval_jaxpr/ppermute | solution.py:17
  319.4 1.9 copy-start.4
  319.4 1.9 copy-start.5
  321.3 1.9 copy-start.8
  323.1 2.9 copy-start.3
  326.0 1.6 copy-start.6
where the time goes:
time: 336 us; the launch traced here: 335 us
  waiting for transfers between devices  192 us (57%)
  matrix products  60.5 us (18%)
  starting transfers between devices  39.9 us (12%)
  local copies, waits for them, and re-layouts  26 us (8%)
  other arithmetic  14.1 us (4%)
    ppermute x15, waiting for transfers between devices, shifted(): return lax.ppermute(x, axis, [(i, (i + by) % peers) for i in range(peers)])  161 us
    all_to_all x1, waiting for transfers between devices, body(): lax.all_to_all(rollout, 'prompt', split_axis=2, concat_axis=0, tiled=True)  30.6 us
    dot_general x34, matrix products, absorb(): jnp.einsum('hrk,kd->hrd', weights.astype(jnp.bfloat16), values, preferred...  30.6 us
    ppermute x15, starting transfers between devices, shifted(): return lax.ppermute(x, axis, [(i, (i + by) % peers) for i in range(peers)])  30.3 us
    dot_general x34, matrix products, absorb(): jnp.einsum('rhd,kd->hrk', queries, key_rows, preferred_element_type=jnp.f...  30 us
    all_to_all x1, starting transfers between devices, body(): lax.all_to_all(rollout, 'prompt', split_axis=2, concat_axis=0, tiled=True)  9.6 us
    while x45, local copies, waits for them, and re-layouts  9.28 us
    reduce_sum x33, other arithmetic, absorb(): row_sum = row_sum * rescale + jnp.sum(weights, axis=-1)  7.97 us
  transfers between devices with their start and end apart: 16, of which 16 were waited for; matrix products, arithmetic and copies ran while one was open for 2% of the time, Pallas kernels for 0%

commit v1 on v0

v1 whole, which is shorter than its diff:
```python
import functools
import math

import jax
import jax.numpy as jnp
from jax import lax
from jax.experimental import pallas as pl
from jax.experimental.pallas import tpu as pltpu
from jax.sharding import PartitionSpec as P

HEAD = 128
MASKED = -1e30
MESH = pl.DeviceIdType.MESH
SCALE2 = HEAD ** (-0.5) * math.log2(math.e)
KEY_TILE = 512


def bit_flips(index, bits):
    return [(1 - 2 * lax.rem(lax.div(index, 1 << b), 2)) * (1 << b) for b in range(bits)]


def flipped(index, flips, mask):
    for b, step in enumerate(flips):
        if mask >> b & 1:
            index = index + step
    return index


def attend_rows(queries, kt, va, s_ref, row0, keys, extra):
    rows = queries.shape[0]
    top = None
    for k0 in range(0, keys, KEY_TILE):
        s = jnp.dot(queries, kt[:, k0 : k0 + KEY_TILE], preferred_element_type=jnp.float32)
        s = extra(k0, s)
        s_ref[row0 : row0 + rows, k0 : k0 + KEY_TILE] = s
        for l0 in range(0, KEY_TILE, 128):
            part = s[:, l0 : l0 + 128]
            top = part if top is None else jnp.maximum(top, part)
    top = jnp.max(top, axis=-1, keepdims=True)
    total = None
    for k0 in range(0, keys, KEY_TILE):
        s = s_ref[row0 : row0 + rows, k0 : k0 + KEY_TILE]
        weights = jnp.exp2((s - top) * SCALE2).astype(jnp.bfloat16)
        part = jnp.dot(weights, va[k0 : k0 + KEY_TILE, :], preferred_element_type=jnp.float32)
        total = part if total is None else total + part
    return (total[:, :HEAD] / total[:, HEAD:]).astype(jnp.bfloat16)


def gather_attend(
    n_prompt, n_ctx, heads,
    prefix_ref, rollout_ref, order_ref, pout_ref, rout_ref,
    pkv, rkv, rq, pq, kt, va, s_ref, bias_ref, gcol, grow,
    local_sem, part_send, part_recv, own_send, own_recv, fwd_send, fwd_recv,
    kv_send, kv_recv, q_send, q_recv,
):
    p = lax.axis_index("prompt")
    c = lax.axis_index("ctx")
    span = heads * HEAD
    width = span + 2 * HEAD
    peers = n_prompt.bit_length() - 1
    flips = bit_flips(p, peers)
    ring = n_ctx // 2
    z, side = lax.div(c, 2), lax.rem(c, 2)
    partner = c + 1 - 2 * side
    rows_peer = rkv.shape[1]
    block = pkv.shape[1]
    prefix_keys = n_ctx * block
    own_keys = n_prompt * rows_peer

    def along(step):
        return lax.rem(z + step, ring) * 2 + side

    barrier = pltpu.get_barrier_semaphore()
    for o in range(1, n_prompt):
        pl.semaphore_signal(barrier, inc=1, device_id=(flipped(p, flips, o), c), device_id_type=MESH)
    pl.semaphore_signal(barrier, inc=1, device_id=(p, partner), device_id_type=MESH)
    for k in range(1, ring):
        pl.semaphore_signal(barrier, inc=1, device_id=(p, along(k)), device_id_type=MESH)

    own_block = prefix_ref.at[0, :, pl.ds(span, 2 * HEAD)]
    local = [
        pltpu.make_async_copy(own_block, pkv.at[c], local_sem.at[0]),
        pltpu.make_async_copy(prefix_ref.at[0, :, pl.ds(0, span)], pq, local_sem.at[1]),
        pltpu.make_async_copy(rollout_ref.at[0, 0, p, :, pl.ds(span, 2 * HEAD)], rkv.at[p], local_sem.at[2]),
        pltpu.make_async_copy(rollout_ref.at[0, 0, p, :, pl.ds(0, span)], rq.at[p], local_sem.at[3]),
    ]
    for copy in local:
        copy.start()

    def to_partner(slot):
        return pltpu.make_async_remote_copy(
            own_block, pkv.at[slot], part_send.at[0], part_recv.at[0], device_id=(p, partner), device_id_type=MESH
        )

    def own_to(k, slot):
        return pltpu.make_async_remote_copy(
            own_block, pkv.at[slot], own_send.at[k], own_recv.at[k], device_id=(p, along(k)), device_id_type=MESH
        )

    def fwd_to(k, slot):
        return pltpu.make_async_remote_copy(
            pkv.at[partner], pkv.at[slot], fwd_send.at[k], fwd_recv.at[k], device_id=(p, along(k)), device_id_type=MESH
        )

    def kv_to(o, slot):
        there = flipped(p, flips, o)
        return pltpu.make_async_remote_copy(
            rollout_ref.at[0, 0, there, :, pl.ds(span, 2 * HEAD)], rkv.at[slot],
            kv_send.at[o], kv_recv.at[o], device_id=(there, c), device_id_type=MESH,
        )

    def q_to(o, slot):
        there = flipped(p, flips, o)
        return pltpu.make_async_remote_copy(
            rollout_ref.at[0, 0, there, :, pl.ds(0, span)], rq.at[slot],
            q_send.at[o], q_recv.at[o], device_id=(there, c), device_id_type=MESH,
        )

    pl.semaphore_wait(barrier, n_prompt - 1 + 1 + ring - 1)
    half = n_prompt // 2
    to_partner(c).start()
    for k in (1, ring - 1, 2, ring - 2, 3, ring - 3, 4):
        own_to(k, c).start()
    for o in list(range(half, n_prompt)) + list(range(half // 2, half)) + list(range(1, half // 2)):
        kv_to(o, p).start()
    for o in range(1, n_prompt):
        q_to(o, p).start()

    order = order_ref[...]
    place = lax.broadcasted_iota(jnp.int32, (128, own_keys), 1).astype(jnp.float32)
    for a0 in range(0, own_keys, 128):
        arrived = lax.broadcasted_iota(jnp.int32, (128, own_keys), 0) + a0
        at = jnp.sum(jnp.where(order == arrived, place, 0.0), axis=-1, keepdims=True)
        at = jnp.broadcast_to(at, (128, 128))
        gcol[a0 : a0 + 128, :] = at
        grow[:, a0 : a0 + 128] = at.T[:8]

    va[:, HEAD:] = jnp.ones((va.shape[0], HEAD), jnp.bfloat16)
    for copy in local:
        copy.wait()

    def take_prefix(slot):
        rows = pl.ds(pl.multiple_of(slot * block, block), block)
        got = pkv[slot]
        kt[:, rows] = got[:, :HEAD].T
        va[rows, :HEAD] = got[:, HEAD:]

    take_prefix(c)
    to_partner(partner).wait_recv()
    for k in (1, ring - 1, 2, ring - 2, 3, ring - 3, 4):
        fwd_to(k, partner).start()
    take_prefix(partner)
    for k in (1, ring - 1, 2, ring - 2, 3, ring - 3, 4):
        slot = along(ring - k)
        own_to(k, slot).wait_recv()
        take_prefix(slot)

    for o in range(1, n_prompt):
        kv_to(o, flipped(p, flips, o)).wait_recv()
    for a0 in range(0, own_keys, 128):
        got = rkv[a0 // rows_peer : (a0 + 128) // rows_peer].reshape(128, 2 * HEAD)
        at = prefix_keys + a0
        kt[:, at : at + 128] = got[:, :HEAD].T
        va[at : at + 128, :HEAD] = got[:, HEAD:]

    for k in (1, ring - 1, 2, ring - 2, 3, ring - 3, 4):
        slot = along(ring - k) + 1 - 2 * side
        fwd_to(k, slot).wait_recv()
        take_prefix(slot)

    position = c * block + lax.rem(lax.broadcasted_iota(jnp.int32, (2 * block, KEY_TILE), 0), block)
    lane = lax.broadcasted_iota(jnp.int32, (2 * block, KEY_TILE), 1)
    for h in range(0, heads, 2):
        queries = jnp.concatenate([pq[:, h * HEAD : (h + 1) * HEAD], pq[:, (h + 1) * HEAD : (h + 2) * HEAD]], axis=0)
        out = attend_rows(
            queries, kt, va, s_ref, h * block, prefix_keys,
            lambda k0, s: jnp.where(lane + k0 <= position, s, MASKED),
        )
        pout_ref[:, h * HEAD : (h + 1) * HEAD] = out[:block]
        pout_ref[:, (h + 1) * HEAD : (h + 2) * HEAD] = out[block:]

    quad = lax.div(p, 4)
    chunk_rows = 4 * rows_peer

    def chunk(i, carry):
        base = 0
        for b in range(peers - 2):
            base = base + lax.rem(lax.div(quad, 1 << b) + lax.div(i, 1 << b), 2) * (1 << b)
        source = base * 4
        for k in range(4):
            @pl.when(i * 4 + k > 0)
            def _():
                from_peer = base * 4 + flipped(lax.rem(p, 4), flips[:2], k)
                pltpu.make_async_remote_copy(
                    rollout_ref.at[0, 0, from_peer, :, pl.ds(0, span)], rq.at[from_peer],
                    q_send.at[i * 4 + k], q_recv.at[i * 4 + k], device_id=(from_peer, c), device_id_type=MESH,
                ).wait_recv()
        row0 = pl.multiple_of(base * chunk_rows, chunk_rows)
        mine = gcol[pl.ds(row0, chunk_rows), :]
        first = jnp.where(mine >= own_keys // 2, float(own_keys // 2), 0.0)
        for k0 in range(0, own_keys, 128):
            other = grow[0:1, k0 : k0 + 128]
            seen = (other <= mine) & (other >= first)
            bias_ref[:, k0 : k0 + 128] = jnp.where(seen, 0.0, MASKED)

        def masked(k0, s):
            if k0 < prefix_keys:
                return s
            bias = bias_ref[:, k0 - prefix_keys : k0 - prefix_keys + KEY_TILE]
            return s + jnp.concatenate([bias, bias], axis=0)

        rows = rq[pl.ds(source, 4)].reshape(chunk_rows, span)
        for h in range(0, heads, 2):
            queries = jnp.concatenate([rows[:, h * HEAD : (h + 1) * HEAD], rows[:, (h + 1) * HEAD : (h + 2) * HEAD]], axis=0)
            out = attend_rows(queries, kt, va, s_ref, h * chunk_rows, prefix_keys + own_keys, masked)
            rout_ref[pl.ds(row0, chunk_rows), h * HEAD : (h + 1) * HEAD] = out[:chunk_rows]
            rout_ref[pl.ds(row0, chunk_rows), (h + 1) * HEAD : (h + 2) * HEAD] = out[chunk_rows:]
        return carry

    lax.fori_loop(0, n_prompt // 4, chunk, 0)

    to_partner(c).wait_send()
    for k in range(1, ring):
        own_to(k, c).wait_send()
        fwd_to(k, partner).wait_send()
    for o in range(1, n_prompt):
        kv_to(o, p).wait_send()
        q_to(o, p).wait_send()


def place_rows(len_ref, order_ref, tmp_ref, ptmp_ref, rout_ref, pout_ref):
    step = pl.program_id(0)
    rows = rout_ref.shape[0]
    total = tmp_ref.shape[0]
    per_resp = total // len_ref.shape[1] // rows

    @pl.when(step == 0)
    def _():
        pout_ref[...] = ptmp_ref[...]

    limit = len_ref[0, lax.div(step, per_resp)] - lax.rem(step, per_resp) * rows
    order = jnp.broadcast_to(order_ref[...], (128, rows)).T
    live = lax.broadcasted_iota(jnp.int32, (rows, 128), 0) < limit
    order = jnp.where(live, order, -1)
    lane = lax.broadcasted_iota(jnp.int32, (rows, 128), 1)
    pick = jnp.concatenate(
        [jnp.where(order == lane + a0, 1.0, 0.0).astype(jnp.bfloat16) for a0 in range(0, total, 128)], axis=1
    )
    rout_ref[...] = jnp.dot(pick, tmp_ref[...], preferred_element_type=jnp.float32).astype(jnp.bfloat16)


def solution(mesh):
    n_prompt, n_ctx = mesh.shape["prompt"], mesh.shape["ctx"]

    def body(prefix_qkv, rollout, arrival_order, resp_len):
        block, width = prefix_qkv.shape[1:]
        rows_peer = rollout.shape[3]
        span = width - 2 * HEAD
        heads = span // HEAD
        own = n_prompt * rows_peer
        keys = n_ctx * block + own
        order = arrival_order.reshape(1, own)
        dma = pltpu.SemaphoreType.DMA
        any_spec = pl.BlockSpec(memory_space=pl.ANY)
        vmem_spec = pl.BlockSpec(memory_space=pltpu.VMEM)
        ptmp, tmp = pl.pallas_call(
            functools.partial(gather_attend, n_prompt, n_ctx, heads),
            out_shape=(
                jax.ShapeDtypeStruct((block, span), jnp.bfloat16),
                jax.ShapeDtypeStruct((own, span), jnp.bfloat16),
            ),
            in_specs=[any_spec, any_spec, vmem_spec],
            out_specs=(vmem_spec, vmem_spec),
            scratch_shapes=[
                pltpu.VMEM((n_ctx, block, 2 * HEAD), jnp.bfloat16),
                pltpu.VMEM((n_prompt, rows_peer, 2 * HEAD), jnp.bfloat16),
                pltpu.VMEM((n_prompt, rows_peer, span), jnp.bfloat16),
                pltpu.VMEM((block, span), jnp.bfloat16),
                pltpu.VMEM((HEAD, keys), jnp.bfloat16),
                pltpu.VMEM((keys, 2 * HEAD), jnp.bfloat16),
                pltpu.VMEM((4 * 128, keys), jnp.float32),
                pltpu.VMEM((4 * rows_peer, own), jnp.float32),
                pltpu.VMEM((own, 128), jnp.float32),
                pltpu.VMEM((8, own), jnp.float32),
                dma((4,)),
                dma((1,)),
                dma((1,)),
                dma((n_ctx // 2,)),
                dma((n_ctx // 2,)),
                dma((n_ctx // 2,)),
                dma((n_ctx // 2,)),
                dma((n_prompt,)),
                dma((n_prompt,)),
                dma((n_prompt,)),
                dma((n_prompt,)),
            ],
            compiler_params=pltpu.CompilerParams(collective_id=0, has_side_effects=True),
            name="gather_attend",
        )(prefix_qkv, rollout, order)
        step_rows = 256
        out, pout = pl.pallas_call(
            place_rows,
            grid=(own // step_rows,),
            out_shape=(
                jax.ShapeDtypeStruct((own, span), jnp.bfloat16),
                jax.ShapeDtypeStruct((block, span), jnp.bfloat16),
            ),
            in_specs=[
                pl.BlockSpec(memory_space=pltpu.SMEM),
                pl.BlockSpec((1, step_rows), lambda i: (0, i)),
                pl.BlockSpec((own, span), lambda i: (0, 0)),
                pl.BlockSpec((block, span), lambda i: (0, 0)),
            ],
            out_specs=(
                pl.BlockSpec((step_rows, span), lambda i: (i, 0)),
                pl.BlockSpec((block, span), lambda i: (0, 0)),
            ),
            name="place_rows",
        )(resp_len, order, tmp, ptmp)
        per = resp_len.shape[1]
        return pout[None], out.reshape(1, per, own // per, span)

    spec = P("prompt", "ctx", None)
    return jax.shard_map(
        body,
        mesh=mesh,
        in_specs=(spec, P("prompt", "ctx", None, None, None), spec, P("prompt", "ctx")),
        out_specs=(spec, P("prompt", "ctx", None, None)),
        check_vma=False,
    )
```

time: 336 us -> 74.1 us (0.22)
  the two profiles are of different devices: /device:TPU:10 before, /device:TPU:1 now
where the time goes in v1:
time: 74.1 us; the launch traced here: 73.9 us
  Pallas kernels  73.3 us (99%)
    pallas_call x1, Pallas kernels, body(): pl.pallas_call(functools.partial(gather_attend, n_prompt, n_ctx, heads),...  68.9 us
    pallas_call x1, Pallas kernels, body(): pl.pallas_call(place_rows, grid=(own // step_rows,), out_shape=(jax.Shape...  4.41 us

profile of v1, /device:TPU:1, one launch (start us, length us, event | category | flops | bytes accessed | tf_op | source)
XLA Modules:
  0.0 73.9 jit_solution(18427186883195718323)
XLA Ops:
  0.6 68.9 %gather_attend.1 = (bf16[128,512]{1,0:T(8,128)(2,1)}, bf16[1024,512]{1,0:T(8,128)(2,1)}) custom-call(bf16[1,128,768]{2,1,0:T(8,128)(2,1)} %prefix_ref.1, bf16[1,1,32,32,768]{4,3,2,1,0:T(8,128)(2,1)} %rollout_ref.1, s32[1,1024]{1,0:T(1,128)} %bitcast.3), custom_call_target="tpu_custom_call" | custom-call | tf_op jit(solution)/shard_map/gather_attend/pallas_call | solution.py:266
  69.5 4.4 %place_rows.1 = (bf16[1024,512]{1,0:T(8,128)(2,1)}, bf16[128,512]{1,0:T(8,128)(2,1)}) custom-call(s32[1,2]{1,0:T(1,128)} %len_ref.1, s32[1,1024]{1,0:T(1,128)} %bitcast.4, bf16[1024,512]{1,0:T(8,128)(2,1)} %get-tuple-element.6.tmp_ref, bf16[128,512]{1,0:T(8,128)(2,1)} %get-tuple-element.7.ptmp_ref), custom_call_target="tpu_custom_call" | custom-call | tf_op jit(solution)/shard_map/place_rows/pallas_call | solution.py:301

commit v2 on v1

--- a/solution.py
+++ b/solution.py
@@ -13,6 +13,8 @@
 MESH = pl.DeviceIdType.MESH
 SCALE2 = HEAD ** (-0.5) * math.log2(math.e)
 KEY_TILE = 512
+UNIT = 2
+NEAR = (1, 7, 2, 6)
 
 
 def bit_flips(index, bits):
@@ -26,31 +28,40 @@
     return index
 
 
-def attend_rows(queries, kt, va, s_ref, row0, keys, extra):
-    rows = queries.shape[0]
-    top = None
-    for k0 in range(0, keys, KEY_TILE):
-        s = jnp.dot(queries, kt[:, k0 : k0 + KEY_TILE], preferred_element_type=jnp.float32)
-        s = extra(k0, s)
-        s_ref[row0 : row0 + rows, k0 : k0 + KEY_TILE] = s
-        for l0 in range(0, KEY_TILE, 128):
-            part = s[:, l0 : l0 + 128]
-            top = part if top is None else jnp.maximum(top, part)
-    top = jnp.max(top, axis=-1, keepdims=True)
-    total = None
-    for k0 in range(0, keys, KEY_TILE):
-        s = s_ref[row0 : row0 + rows, k0 : k0 + KEY_TILE]
-        weights = jnp.exp2((s - top) * SCALE2).astype(jnp.bfloat16)
-        part = jnp.dot(weights, va[k0 : k0 + KEY_TILE, :], preferred_element_type=jnp.float32)
-        total = part if total is None else total + part
-    return (total[:, :HEAD] / total[:, HEAD:]).astype(jnp.bfloat16)
+def score_tile(queries, kt, s_ref, k0, top, extra):
+    s = jnp.dot(queries, kt[:, k0 : k0 + KEY_TILE], preferred_element_type=jnp.float32)
+    s = extra(k0, s)
+    s_ref[:, k0 : k0 + KEY_TILE] = s
+    for l0 in range(0, KEY_TILE, 128):
+        part = s[:, l0 : l0 + 128]
+        top = part if top is None else jnp.maximum(top, part)
+    return top
+
+
+def weigh_tile(va, s_ref, k0, top, carried):
+    weights = jnp.exp2((s_ref[:, k0 : k0 + KEY_TILE] - top) * SCALE2)
+    row_sum, total = carried
+    for l0 in range(0, KEY_TILE, 128):
+        part = weights[:, l0 : l0 + 128]
+        row_sum = part if row_sum is None else row_sum + part
+    part = jnp.dot(weights.astype(jnp.bfloat16), va[k0 : k0 + KEY_TILE, :], preferred_element_type=jnp.float32)
+    return row_sum, part if total is None else total + part
+
+
+def finish_rows(carried):
+    row_sum, total = carried
+    return (total / jnp.sum(row_sum, axis=-1, keepdims=True)).astype(jnp.bfloat16)
+
+
+def stack_heads(rows, h):
+    return jnp.concatenate([rows[:, g * HEAD : (g + 1) * HEAD] for g in range(h, h + UNIT)], axis=0)
 
 
 def gather_attend(
     n_prompt, n_ctx, heads,
     prefix_ref, rollout_ref, order_ref, pout_ref, rout_ref,
-    pkv, rkv, rq, pq, kt, va, s_ref, bias_ref, gcol, grow,
-    local_sem, part_send, part_recv, own_send, own_recv, fwd_send, fwd_recv,
+    pkv, rkv, rq, pq, kt, va, s_ref, top_ref, bias_ref, gcol, grow,
+    local_sem, part_send, part_recv, own_send, own_recv, fwd_send, fwd_recv, own_hop_send, own_hop_recv, fwd_hop_send, fwd_hop_recv,
     kv_send, kv_recv, q_send, q_recv,
 ):
     p = lax.axis_index("prompt")
@@ -74,7 +85,7 @@
     for o in range(1, n_prompt):
         pl.semaphore_signal(barrier, inc=1, device_id=(flipped(p, flips, o), c), device_id_type=MESH)
     pl.semaphore_signal(barrier, inc=1, device_id=(p, partner), device_id_type=MESH)
-    for k in range(1, ring):
+    for k in NEAR:
         pl.semaphore_signal(barrier, inc=1, device_id=(p, along(k)), device_id_type=MESH)
 
     own_block = prefix_ref.at[0, :, pl.ds(span, 2 * HEAD)]
@@ -102,6 +113,23 @@
             pkv.at[partner], pkv.at[slot], fwd_send.at[k], fwd_recv.at[k], device_id=(p, along(k)), device_id_type=MESH
         )
 
+    def hop_copies(own, arrived):
+        slot = along if own else (lambda k: along(k) + 1 - 2 * side)
+        send, recv = (own_hop_send, own_hop_recv) if own else (fwd_hop_send, fwd_hop_recv)
+        half = block // 2
+        low, high = pl.ds(0, half), pl.ds(half, half)
+        before, after = pkv.at[slot(ring - 2)], pkv.at[slot(2)]
+        ends = [before, before.at[low], after, after.at[high]]
+        if arrived:
+            ends = [pkv.at[slot(ring - 3)], pkv.at[slot(4), low], pkv.at[slot(3)], pkv.at[slot(4), high]]
+        starts = [before, before.at[low], after, after.at[high]]
+        return [
+            pltpu.make_async_remote_copy(
+                start, end, send.at[j], recv.at[j], device_id=(p, along(k)), device_id_type=MESH
+            )
+            for j, (start, end, k) in enumerate(zip(starts, ends, (1, 2, ring - 1, ring - 2)))
+        ]
+
     def kv_to(o, slot):
         there = flipped(p, flips, o)
         return pltpu.make_async_remote_copy(
@@ -115,16 +143,6 @@
             rollout_ref.at[0, 0, there, :, pl.ds(0, span)], rq.at[slot],
             q_send.at[o], q_recv.at[o], device_id=(there, c), device_id_type=MESH,
         )
-
-    pl.semaphore_wait(barrier, n_prompt - 1 + 1 + ring - 1)
-    half = n_prompt // 2
-    to_partner(c).start()
-    for k in (1, ring - 1, 2, ring - 2, 3, ring - 3, 4):
-        own_to(k, c).start()
-    for o in list(range(half, n_prompt)) + list(range(half // 2, half)) + list(range(1, half // 2)):
-        kv_to(o, p).start()
-    for o in range(1, n_prompt):
-        q_to(o, p).start()
 
     order = order_ref[...]
     place = lax.broadcasted_iota(jnp.int32, (128, own_keys), 1).astype(jnp.float32)
@@ -135,7 +153,16 @@
         gcol[a0 : a0 + 128, :] = at
         grow[:, a0 : a0 + 128] = at.T[:8]
 
-    va[:, HEAD:] = jnp.ones((va.shape[0], HEAD), jnp.bfloat16)
+    pl.semaphore_wait(barrier, n_prompt + len(NEAR))
+    half = n_prompt // 2
+    to_partner(c).start()
+    for k in NEAR:
+        own_to(k, c).start()
+    for o in list(range(half, n_prompt)) + list(range(half // 2, half)) + list(range(1, half // 2)):
+        kv_to(o, p).start()
+    for o in range(1, n_prompt):
+        q_to(o, p).start()
+
     for copy in local:
         copy.wait()
 
@@ -143,50 +170,85 @@
         rows = pl.ds(pl.multiple_of(slot * block, block), block)
         got = pkv[slot]
         kt[:, rows] = got[:, :HEAD].T
-        va[rows, :HEAD] = got[:, HEAD:]
+        va[rows, :] = got[:, HEAD:]
+
+    def other(k):
+        return along(k) + 1 - 2 * side
 
     take_prefix(c)
     to_partner(partner).wait_recv()
-    for k in (1, ring - 1, 2, ring - 2, 3, ring - 3, 4):
+    for k in NEAR:
         fwd_to(k, partner).start()
+    own_hops = hop_copies(True, False)
+    own_to(2, along(ring - 2)).wait_recv()
+    own_hops[0].start()
+    own_hops[1].start()
+    own_to(ring - 2, along(2)).wait_recv()
+    own_hops[2].start()
+    own_hops[3].start()
     take_prefix(partner)
-    for k in (1, ring - 1, 2, ring - 2, 3, ring - 3, 4):
-        slot = along(ring - k)
-        own_to(k, slot).wait_recv()
-        take_prefix(slot)
-
+    take_prefix(along(2))
+    take_prefix(along(ring - 2))
+    for k in (1, ring - 1):
+        own_to(k, along(ring - k)).wait_recv()
+        take_prefix(along(ring - k))
+    fwd_hops = hop_copies(False, False)
+    fwd_to(2, other(ring - 2)).wait_recv()
+    fwd_hops[0].start()
+    fwd_hops[1].start()
+    fwd_to(ring - 2, other(2)).wait_recv()
+    fwd_hops[2].start()
+    fwd_hops[3].start()
+    take_prefix(other(2))
+    take_prefix(other(ring - 2))
+    for k in (1, ring - 1):
+        fwd_to(k, other(ring - k)).wait_recv()
+        take_prefix(other(ring - k))
     for o in range(1, n_prompt):
         kv_to(o, flipped(p, flips, o)).wait_recv()
     for a0 in range(0, own_keys, 128):
         got = rkv[a0 // rows_peer : (a0 + 128) // rows_peer].reshape(128, 2 * HEAD)
         at = prefix_keys + a0
         kt[:, at : at + 128] = got[:, :HEAD].T
-        va[at : at + 128, :HEAD] = got[:, HEAD:]
-
-    for k in (1, ring - 1, 2, ring - 2, 3, ring - 3, 4):
-        slot = along(ring - k) + 1 - 2 * side
-        fwd_to(k, slot).wait_recv()
-        take_prefix(slot)
-
-    position = c * block + lax.rem(lax.broadcasted_iota(jnp.int32, (2 * block, KEY_TILE), 0), block)
-    lane = lax.broadcasted_iota(jnp.int32, (2 * block, KEY_TILE), 1)
-    for h in range(0, heads, 2):
-        queries = jnp.concatenate([pq[:, h * HEAD : (h + 1) * HEAD], pq[:, (h + 1) * HEAD : (h + 2) * HEAD]], axis=0)
-        out = attend_rows(
-            queries, kt, va, s_ref, h * block, prefix_keys,
-            lambda k0, s: jnp.where(lane + k0 <= position, s, MASKED),
-        )
-        pout_ref[:, h * HEAD : (h + 1) * HEAD] = out[:block]
-        pout_ref[:, (h + 1) * HEAD : (h + 2) * HEAD] = out[block:]
+        va[at : at + 128, :] = got[:, HEAD:]
+    for own in (True, False):
+        for copy in hop_copies(own, True):
+            copy.wait_recv()
+        for k in (3, 4, 5):
+            take_prefix(along(k) if own else other(k))
+
+    position = c * block + lax.rem(lax.broadcasted_iota(jnp.int32, (UNIT * block, KEY_TILE), 0), block)
+    lane = lax.broadcasted_iota(jnp.int32, (UNIT * block, KEY_TILE), 1)
+
+    def causal(k0, s):
+        return jnp.where(lane + k0 <= position, s, MASKED)
+
+    for h in range(0, heads, UNIT):
+        queries = stack_heads(pq, h)
+        top = None
+        for k0 in range(0, prefix_keys, KEY_TILE):
+            top = score_tile(queries, kt, s_ref.at[0], k0, top, causal)
+        top = jnp.max(top, axis=-1, keepdims=True)
+        carried = None, None
+        for k0 in range(0, prefix_keys, KEY_TILE):
+            carried = weigh_tile(va, s_ref.at[0], k0, top, carried)
+        out = finish_rows(carried)
+        for g in range(UNIT):
+            pout_ref[:, (h + g) * HEAD : (h + g + 1) * HEAD] = out[g * block : (g + 1) * block]
 
     quad = lax.div(p, 4)
     chunk_rows = 4 * rows_peer
-
-    def chunk(i, carry):
+    chunks = n_prompt // 4
+    keys = prefix_keys + own_keys
+
+    def base_of(i):
         base = 0
         for b in range(peers - 2):
             base = base + lax.rem(lax.div(quad, 1 << b) + lax.div(i, 1 << b), 2) * (1 << b)
-        source = base * 4
+        return base
+
+    def get_chunk(i):
+        base = base_of(i)
         for k in range(4):
             @pl.when(i * 4 + k > 0)
             def _():
@@ -195,34 +257,66 @@
                     rollout_ref.at[0, 0, from_peer, :, pl.ds(0, span)], rq.at[from_peer],
                     q_send.at[i * 4 + k], q_recv.at[i * 4 + k], device_id=(from_peer, c), device_id_type=MESH,
                 ).wait_recv()
-        row0 = pl.multiple_of(base * chunk_rows, chunk_rows)
-        mine = gcol[pl.ds(row0, chunk_rows), :]
+        mine = gcol[pl.ds(pl.multiple_of(base * chunk_rows, chunk_rows), chunk_rows), :]
         first = jnp.where(mine >= own_keys // 2, float(own_keys // 2), 0.0)
         for k0 in range(0, own_keys, 128):
             other = grow[0:1, k0 : k0 + 128]
             seen = (other <= mine) & (other >= first)
             bias_ref[:, k0 : k0 + 128] = jnp.where(seen, 0.0, MASKED)
 
-        def masked(k0, s):
-            if k0 < prefix_keys:
-                return s
-            bias = bias_ref[:, k0 - prefix_keys : k0 - prefix_keys + KEY_TILE]
-            return s + jnp.concatenate([bias, bias], axis=0)
-
-        rows = rq[pl.ds(source, 4)].reshape(chunk_rows, span)
-        for h in range(0, heads, 2):
-            queries = jnp.concatenate([rows[:, h * HEAD : (h + 1) * HEAD], rows[:, (h + 1) * HEAD : (h + 2) * HEAD]], axis=0)
-            out = attend_rows(queries, kt, va, s_ref, h * chunk_rows, prefix_keys + own_keys, masked)
-            rout_ref[pl.ds(row0, chunk_rows), h * HEAD : (h + 1) * HEAD] = out[:chunk_rows]
-            rout_ref[pl.ds(row0, chunk_rows), (h + 1) * HEAD : (h + 2) * HEAD] = out[chunk_rows:]
-        return carry
-
-    lax.fori_loop(0, n_prompt // 4, chunk, 0)
+    def masked(k0, s):
+        if k0 < prefix_keys:
+            return s
+        bias = bias_ref[:, k0 - prefix_keys : k0 - prefix_keys + KEY_TILE]
+        return s + jnp.concatenate([bias] * UNIT, axis=0)
+
+    def queries_of(i, h):
+        return stack_heads(rq[pl.ds(base_of(i) * 4, 4)].reshape(chunk_rows, span), h)
+
+    get_chunk(0)
+    queries = queries_of(0, 0)
+    top = None
+    for k0 in range(0, keys, KEY_TILE):
+        top = score_tile(queries, kt, s_ref.at[0], k0, top, masked)
+    top_ref[...] = jnp.broadcast_to(jnp.max(top, axis=-1, keepdims=True), top.shape)
+
+    def chunk(i, last):
+        row0 = pl.multiple_of(base_of(i) * chunk_rows, chunk_rows)
+        units = heads // UNIT
+        for u in range(units):
+            ahead = not (last and u == units - 1)
+            if not ahead:
+                pass
+            elif u == units - 1:
+                get_chunk(i + 1)
+                queries = queries_of(i + 1, 0)
+            else:
+                queries = queries_of(i, (u + 1) * UNIT)
+            now_top = top_ref[:, 0:1]
+            top, carried = None, (None, None)
+            for k0 in range(0, keys, KEY_TILE):
+                if ahead:
+                    top = score_tile(queries, kt, s_ref.at[(u + 1) % 2], k0, top, masked)
+                carried = weigh_tile(va, s_ref.at[u % 2], k0, now_top, carried)
+            if ahead:
+                top_ref[...] = jnp.broadcast_to(jnp.max(top, axis=-1, keepdims=True), top.shape)
+            out = finish_rows(carried)
+            for g in range(UNIT):
+                h = u * UNIT + g
+                rout_ref[pl.ds(row0, chunk_rows), h * HEAD : (h + 1) * HEAD] = out[g * chunk_rows : (g + 1) * chunk_rows]
+
+    @pl.loop(0, chunks - 1)
+    def _(i):
+        chunk(i, False)
+
+    chunk(chunks - 1, True)
 
     to_partner(c).wait_send()
-    for k in range(1, ring):
+    for k in NEAR:
         own_to(k, c).wait_send()
         fwd_to(k, partner).wait_send()
+    for copy in own_hops + fwd_hops:
+        copy.wait_send()
     for o in range(1, n_prompt):
         kv_to(o, p).wait_send()
         q_to(o, p).wait_send()
@@ -277,8 +371,9 @@
                 pltpu.VMEM((n_prompt, rows_peer, span), jnp.bfloat16),
                 pltpu.VMEM((block, span), jnp.bfloat16),
                 pltpu.VMEM((HEAD, keys), jnp.bfloat16),
-                pltpu.VMEM((keys, 2 * HEAD), jnp.bfloat16),
-                pltpu.VMEM((4 * 128, keys), jnp.float32),
+                pltpu.VMEM((keys, HEAD), jnp.bfloat16),
+                pltpu.VMEM((2, UNIT * 128, keys), jnp.float32),
+                pltpu.VMEM((UNIT * 128, 128), jnp.float32),
                 pltpu.VMEM((4 * rows_peer, own), jnp.float32),
                 pltpu.VMEM((own, 128), jnp.float32),
                 pltpu.VMEM((8, own), jnp.float32),
@@ -289,6 +384,10 @@
                 dma((n_ctx // 2,)),
                 dma((n_ctx // 2,)),
                 dma((n_ctx // 2,)),
+                dma((4,)),
+                dma((4,)),
+                dma((4,)),
+                dma((4,)),
                 dma((n_prompt,)),
                 dma((n_prompt,)),
                 dma((n_prompt,)),

time: 74.1 us -> 65.9 us (0.89)
  Pallas kernels: 73.3 us -> 64.9 us
    pallas_call x1, Pallas kernels: 68.9 us -> 60.5 us  [body(): pl.pallas_call(functools.partial(gather_attend, n_prompt, n_ctx, heads),...]
where the time goes in v2:
time: 65.9 us; the launch traced here: 65.5 us
  Pallas kernels  64.9 us (98%)
    pallas_call x1, Pallas kernels, body(): pl.pallas_call(functools.partial(gather_attend, n_prompt, n_ctx, heads),...  60.5 us
    pallas_call x1, Pallas kernels, body(): pl.pallas_call(place_rows, grid=(own // step_rows,), out_shape=(jax.Shape...  4.41 us

profile of v2, /device:TPU:1, one launch (start us, length us, event | category | flops | bytes accessed | tf_op | source)
XLA Modules:
  0.0 65.5 jit_solution(13473537435020454606)
XLA Ops:
  0.6 60.5 %gather_attend.1 = (bf16[128,512]{1,0:T(8,128)(2,1)}, bf16[1024,512]{1,0:T(8,128)(2,1)}) custom-call(bf16[1,128,768]{2,1,0:T(8,128)(2,1)} %prefix_ref.1, bf16[1,1,32,32,768]{4,3,2,1,0:T(8,128)(2,1)} %rollout_ref.1, s32[1,1024]{1,0:T(1,128)} %bitcast.3), custom_call_target="tpu_custom_call" | custom-call | tf_op jit(solution)/shard_map/gather_attend/pallas_call | solution.py:360
  61.1 4.4 %place_rows.1 = (bf16[1024,512]{1,0:T(8,128)(2,1)}, bf16[128,512]{1,0:T(8,128)(2,1)}) custom-call(s32[1,2]{1,0:T(1,128)} %len_ref.1, s32[1,1024]{1,0:T(1,128)} %bitcast.4, bf16[1024,512]{1,0:T(8,128)(2,1)} %get-tuple-element.6.tmp_ref, bf16[128,512]{1,0:T(8,128)(2,1)} %get-tuple-element.7.ptmp_ref), custom_call_target="tpu_custom_call" | custom-call | tf_op jit(solution)/shard_map/place_rows/pallas_call | solution.py:400
